TPU v7x, 32 devices: a whole 2x2x4 slice. The times are simulated.
32 devices in a mesh: section: 2 (over core), req: 4 (over z), head: 4 (over y, x).
Axes of the slice: x: 2, y: 2, z: 4, core: 2. Of those that a mesh axis runs over, the one named last changes fastest.
Arguments:
- tokens: bfloat16 [128, 1024], P('req'), may hold values from -60 to 60, as said below
- deal: int32 [128], P('req'), may hold values from 0 to 127, each once
- lengths: int32 [2, 128], P('section', 'req'), may hold values from 2 to 256, as said below
- cache_keys: bfloat16 [2, 128, 256, 1024], P('section', 'req', None, 'head'), may hold values from -1024 to 1024
- cache_values: bfloat16 [2, 128, 256, 1024], P('section', 'req', None, 'head'), may hold values from -6 to 6
- w_qkv: bfloat16 [2, 1024, 3, 1024], P('section', None, None, 'head'), may hold values from -0.1875 to 0.1875
- w_out: bfloat16 [2, 1024, 1024], P('section', 'head'), may hold values from -0.1875 to 0.1875
- attn_gain: float32 [2, 1024], P('section'), may hold values from 0.5 to 1.5
- ffn_gain: float32 [2, 1024], P('section'), may hold values from 0.5 to 1.5
- w_gate: bfloat16 [2, 1024, 45056], P('section', None, ('req', 'head')), may hold values from -0.1875 to 0.1875
- w_up: bfloat16 [2, 1024, 45056], P('section', None, ('req', 'head')), may hold values from -0.1875 to 0.1875
- w_down: bfloat16 [2, 45056, 1024], P('section', ('req', 'head')), may hold values from -0.109375 to 0.109375
- routes: int32 [2, 128, 2], P('section', 'req'), may hold values from 0 to 15, all different within a row; in each aligned block of 16 rows (0 to 15, 16 to 31, ..., all dimensions but the last counted through in order) at most 4 rows name the same one
- gates: bfloat16 [2, 128, 2], P('section', 'req'), may hold values from 0.25 to 1
Outputs:
- layer_out: bfloat16 [2, 128, 1024], P('section', 'req')
Inputs may be any that keep to these rules, and one draw needn't show every extreme that they name: `tokens`: hidden states with row and feature scales that differ. `deal`: each of 0 to 127 appears once. `lengths`: in each layer, one of the 32 slots of each index of req holds a length of exactly 256; the others are anywhere from 2 to 256. `routes`: the two experts of a slot differ; in each aligned block of 16 slots of one layer no expert is named more than 4 times.
All inputs are finite; a program needn't handle non-finite values.
Results may differ from a plain program's by a relative error of at most 0.0053.
Values may be sent and summed in bfloat16 or wider, within the bound.
A program may use at most 128 MiB of HBM per device.

v0:
```python
import math
import jax
import jax.numpy as jnp
from jax import lax
from jax.sharding import PartitionSpec as P

HEAD_DIM = 64
EXPERTS = 16
FF = 2816
MICRO = 2
epsilon = 1e-06


def shifted(x, axis, by):
    size = lax.axis_size(axis)
    pairs = [(i, i + by) for i in range(size) if 0 <= i + by < size]
    return lax.ppermute(x, axis, pairs)


def rms_scale(values, gain_row):
    mean_square = jnp.mean(values * values, axis=-1, keepdims=True)
    return values * lax.rsqrt(mean_square + epsilon) * gain_row


def attend_block(queries, new_keys, new_values, key_cache, value_cache, lengths):
    score_scale = 1.0 / math.sqrt(queries.shape[-1])
    scores = (
        jnp.einsum("bhd,bjhd->bhj", queries, key_cache, preferred_element_type=jnp.float32)
        * score_scale
    )
    own_score = (
        jnp.sum(queries.astype(jnp.float32) * new_keys.astype(jnp.float32), axis=-1) * score_scale
    )
    positions = jnp.arange(key_cache.shape[1], dtype=jnp.int32)
    in_range = positions[None, None, :] < lengths[:, None, None]
    scores = jnp.where(in_range, scores, -jnp.inf)
    peak_score = jnp.maximum(jnp.max(scores, axis=-1), own_score)
    cache_weight = jnp.exp(scores - peak_score[..., None])
    own_weight = jnp.exp(own_score - peak_score)
    denominator = jnp.sum(cache_weight, axis=-1) + own_weight
    cache_prob = (cache_weight / denominator[..., None]).astype(jnp.bfloat16)
    own_prob = (own_weight / denominator).astype(jnp.bfloat16)
    attended = jnp.einsum(
        "bhj,bjhd->bhd", cache_prob, value_cache, preferred_element_type=jnp.float32
    )
    attended = attended + own_prob.astype(jnp.float32)[..., None] * new_values.astype(jnp.float32)
    return attended.astype(jnp.bfloat16)


def on_device(
    tokens,
    deal,
    lengths,
    cache_keys,
    cache_values,
    w_qkv,
    w_out,
    attn_gain,
    ffn_gain,
    w_gate,
    w_up,
    w_down,
    routes,
    gates,
):
    req_count = lax.axis_size("req")
    head_count = lax.axis_size("head")
    section_index = lax.axis_index("section")
    request_slots = tokens.shape[0]
    model_width = tokens.shape[1]
    block_rows = request_slots // MICRO
    unit_count = w_gate.shape[2]
    head_cols = w_out.shape[1]
    heads_here = head_cols // HEAD_DIM
    context = cache_keys.shape[2]
    expert_ids = jnp.arange(EXPERTS, dtype=jnp.int32)
    own_expert = (lax.axis_index("req") * head_count + lax.axis_index("head")) * unit_count // FF
    qkv_weight = w_qkv[0].reshape(model_width, 3 * head_cols)
    everything = lax.all_gather(tokens, "req", axis=0, tiled=True)
    dealt_rows = jnp.take(everything, deal, axis=0)
    results = jnp.zeros((request_slots, model_width), jnp.bfloat16)
    incoming = jnp.zeros((block_rows, model_width), jnp.bfloat16)
    for tick_index in range(MICRO + 1):
        micro_index = tick_index - section_index
        in_window = (micro_index >= 0) & (micro_index < MICRO)
        clamped = jnp.clip(micro_index, 0, MICRO - 1)
        fresh_rows = lax.dynamic_slice_in_dim(dealt_rows, clamped * block_rows, block_rows, 0)
        hidden_in = jnp.where(section_index == 0, fresh_rows, incoming)
        row_start = clamped * block_rows
        lengths_here = lax.dynamic_slice_in_dim(lengths[0], row_start, block_rows, 0)
        key_cache = lax.dynamic_slice_in_dim(cache_keys[0], row_start, block_rows, 0).reshape(
            block_rows, context, heads_here, HEAD_DIM
        )
        value_cache = lax.dynamic_slice_in_dim(cache_values[0], row_start, block_rows, 0).reshape(
            block_rows, context, heads_here, HEAD_DIM
        )
        route_ids = lax.dynamic_slice_in_dim(routes[0], row_start, block_rows, 0)
        gate_vals = lax.dynamic_slice_in_dim(gates[0], row_start, block_rows, 0)
        normed = rms_scale(hidden_in.astype(jnp.float32), attn_gain[0]).astype(jnp.bfloat16)
        projected = jnp.dot(normed, qkv_weight, preferred_element_type=jnp.float32).astype(
            jnp.bfloat16
        )
        queries = projected[:, :head_cols].reshape(block_rows, heads_here, HEAD_DIM)
        new_keys = projected[:, head_cols : 2 * head_cols].reshape(block_rows, heads_here, HEAD_DIM)
        new_values = projected[:, 2 * head_cols :].reshape(block_rows, heads_here, HEAD_DIM)
        attended = attend_block(
            queries, new_keys, new_values, key_cache, value_cache, lengths_here
        ).reshape(block_rows, head_cols)
        partial_value = jnp.dot(attended, w_out[0], preferred_element_type=jnp.float32)
        attention = lax.psum(partial_value, "head")
        residual = hidden_in.astype(jnp.float32) + attention
        normed_ffn = rms_scale(residual, ffn_gain[0]).astype(jnp.bfloat16)
        bf_zero = jnp.zeros((), jnp.bfloat16)
        combine = jnp.sum(
            jnp.where(
                route_ids[:, :, None] == expert_ids[None, None, :], gate_vals[:, :, None], bf_zero
            ),
            axis=1,
        )
        piece_tokens, piece_combine = lax.all_gather(
            (normed_ffn, combine), "req", axis=0, tiled=True
        )
        expert_row_weight = jnp.sum(
            jnp.where(expert_ids[None, :] == own_expert, piece_combine.astype(jnp.float32), 0.0),
            axis=1,
        )
        gate_part = jnp.dot(piece_tokens, w_gate[0], preferred_element_type=jnp.float32)
        up_part = jnp.dot(piece_tokens, w_up[0], preferred_element_type=jnp.float32)
        hidden = (
            expert_row_weight[:, None] * jax.nn.gelu(gate_part, approximate=True) * up_part
        ).astype(jnp.bfloat16)
        partial_terms = jnp.dot(hidden, w_down[0], preferred_element_type=jnp.float32)
        mixture = lax.psum_scatter(partial_terms, "req", scatter_dimension=0, tiled=True)
        mixture = lax.psum(mixture, "head")
        produced = (residual + mixture).astype(jnp.bfloat16)
        updated = lax.dynamic_update_slice_in_dim(results, produced, clamped * block_rows, 0)
        results = jnp.where(in_window, updated, results)
        if tick_index < MICRO:
            incoming = shifted(produced, "section", 1)
    placed = (
        jnp.zeros((request_slots * req_count, model_width), jnp.float32)
        .at[deal]
        .set(results.astype(jnp.float32))
    )
    initial_rows = lax.psum_scatter(
        placed.astype(jnp.bfloat16), "req", scatter_dimension=0, tiled=True
    )
    return initial_rows[None]


def solution(mesh):
    return jax.shard_map(
        on_device,
        mesh=mesh,
        in_specs=(
            P("req", None),
            P("req"),
            P("section", "req"),
            P("section", "req", None, "head"),
            P("section", "req", None, "head"),
            P("section", None, None, "head"),
            P("section", "head", None),
            P("section", None),
            P("section", None),
            P("section", None, ("req", "head")),
            P("section", None, ("req", "head")),
            P("section", ("req", "head"), None),
            P("section", "req", None),
            P("section", "req", None),
        ),
        out_specs=P("section", "req", None),
        check_vma=False,
    )
```

profile of v0, /device:TPU:0, one launch (start us, length us, event | category | flops | bytes accessed | tf_op | source)
XLA Modules:
  0.0 505.5 jit_solution(13057923560571487558)
XLA Ops:
  7.9 15.8 %all_gather.21 = bf16[128,1024]{1,0:T(8,128)(2,1)S(1)} all-gather(bf16[32,1024]{1,0:T(8,128)(2,1)} %param.14), channel_id=1, replica_groups=mesh['section'=2,'req'=4,'head'=4] {'req'}, dimensions={0}, use_global_device_ids=true | all-gather | bytes 327680 | tf_op jit(solution)/shard_map/all_gather | solution.py:79
  27.1 9.2 %constant_dynamic-slice_fusion.2 = (bf16[1,16,256,256]{3,2,1,0:T(8,128)(2,1)}, bf16[1,16,256,256]{3,2,1,0:T(8,128)(2,1)}, bf16[1,16,256,256]{3,2,1,0:T(8,128)(2,...) fusion(bf16[1,32,256,256]{3,2,1,0:T(8,128)(2,1)} %param.18, ...), kind=kLoop, calls=%fused_computation.162 | loop fusion | bytes 25165836 | tf_op jit(solution)/shard_map/dynamic_slice | solution.py:94
  43.0 3.9 copy.79
  50.7 13.2 %all_gather.22 = bf16[64,16]{1,0:T(8,128)(2,1)S(1)} all-gather(bf16[16,16]{1,0:T(8,128)(2,1)S(1)} %fusion.130), channel_id=1, replica_groups=mesh['section'=2,'req'=4,'head'=4] {'req'}, dimensions={0}, use_global_device_ids=true | all-gather | bytes 2560 | tf_op jit(solution)/shard_map/all_gather | solution.py:120
  64.0 13.1 %all_gather.24 = bf16[64,16]{1,0:T(8,128)(2,1)S(1)} all-gather(bf16[16,16]{1,0:T(8,128)(2,1)S(1)} %fusion.129), channel_id=1, replica_groups=mesh['section'=2,'req'=4,'head'=4] {'req'}, dimensions={0}, use_global_device_ids=true | all-gather | bytes 2560 | tf_op jit(solution)/shard_map/all_gather | solution.py:120
  77.2 13.1 %all_gather.26 = bf16[64,16]{1,0:T(8,128)(2,1)S(1)} all-gather(bf16[16,16]{1,0:T(8,128)(2,1)S(1)} %fusion.128), channel_id=1, replica_groups=mesh['section'=2,'req'=4,'head'=4] {'req'}, dimensions={0}, use_global_device_ids=true | all-gather | bytes 2560 | tf_op jit(solution)/shard_map/all_gather | solution.py:120
  95.5 13.5 %all_gather.23 = bf16[64,1024]{1,0:T(8,128)(2,1)S(1)} all-gather(bf16[16,1024]{1,0:T(8,128)(2,1)S(1)} %multiply_convert_fusion.2), channel_id=1, replica_groups=mesh['section'=2,'req'=4,'head'=4] {'req'}, dimensions={0}, use_global_device_ids=true | all-gather | bytes 163840 | tf_op jit(solution)/shard_map/all_gather | solution.py:120
  112.9 7.2 %fusion.4 = f32[64,1024]{1,0:T(8,128)} fusion(bf16[1,2816,1024]{2,1,0:T(8,128)(2,1)} %param.25, f32[64,2816]{1,0:T(8,128)S(1)} %fusion.45, bf16[64,1024]{1,0:T(8,128)(2,1)S(1)} %all_gather.23, bf16[1,1024,2816]{2,1,0:T(8,128)(2,1)} %param.24), kind=kOutput, calls=%fused_computation.6 | convolution fusion | flops 738557952 | bytes 12648448 | tf_op jit(solution)/shard_map/dot_general | solution.py:132
  120.1 19.8 %reduce-scatter.5.cloned.1.call-done = f32[16,1024]{1,0:T(8,128)} async-done(((f32[64,1024]{1,0:T(8,128)}), f32[16,1024]{1,0:T(8,128)}) %reduce-scatter.5.cloned.1.call-update) | async-done | bytes 65552 | tf_op jit(solution)/shard_map/reduce_scatter | solution.py:133
  140.0 42.5 %all-reduce.9.cloned.1.call-done = f32[16,1024]{1,0:T(8,128)} async-done(((f32[16,1024]{1,0:T(8,128)}), f32[16,1024]{1,0:T(8,128)}) %all-reduce.9.cloned.1.call-update) | async-done | bytes 65552 | tf_op jit(solution)/shard_map/psum | solution.py:134
  188.7 3.9 copy.81
  199.7 41.6 %all-reduce.11.cloned.1.call-done = f32[16,1024]{1,0:T(8,128)} async-done(((f32[16,1024]{1,0:T(8,128)}), f32[16,1024]{1,0:T(8,128)}) %all-reduce.11.cloned.1.call-update) | async-done | bytes 65552 | tf_op jit(solution)/shard_map/psum | solution.py:110
  243.1 13.5 %all_gather.25 = bf16[64,1024]{1,0:T(8,128)(2,1)S(1)} all-gather(bf16[16,1024]{1,0:T(8,128)(2,1)S(1)} %multiply_convert_fusion.1), channel_id=1, replica_groups=mesh['section'=2,'req'=4,'head'=4] {'req'}, dimensions={0}, use_global_device_ids=true | all-gather | bytes 163840 | tf_op jit(solution)/shard_map/all_gather | solution.py:120
  260.5 7.2 %fusion.2 = f32[64,1024]{1,0:T(8,128)} fusion(bf16[1,2816,1024]{2,1,0:T(8,128)(2,1)} %param.25, f32[64,2816]{1,0:T(8,128)S(1)} %fusion.57, bf16[64,1024]{1,0:T(8,128)(2,1)S(1)} %all_gather.25, bf16[1,1024,2816]{2,1,0:T(8,128)(2,1)} %param.24), kind=kOutput, calls=%fused_computation.4 | convolution fusion | flops 738557952 | bytes 12648448 | tf_op jit(solution)/shard_map/dot_general | solution.py:132
  267.7 19.7 %reduce-scatter.7.cloned.1.call-done = f32[16,1024]{1,0:T(8,128)} async-done(((f32[64,1024]{1,0:T(8,128)}), f32[16,1024]{1,0:T(8,128)}) %reduce-scatter.7.cloned.1.call-update) | async-done | bytes 65552 | tf_op jit(solution)/shard_map/reduce_scatter | solution.py:133
  287.5 42.6 %all-reduce.13.cloned.1.call-done = f32[16,1024]{1,0:T(8,128)} async-done(((f32[16,1024]{1,0:T(8,128)}), f32[16,1024]{1,0:T(8,128)}) %all-reduce.13.cloned.1.call-update) | async-done | bytes 65552 | tf_op jit(solution)/shard_map/psum | solution.py:134
  332.6 3.9 copy.82
  336.5 3.9 copy.83
  346.0 41.6 %all-reduce.15.cloned.1.call-done = f32[16,1024]{1,0:T(8,128)} async-done(((f32[16,1024]{1,0:T(8,128)}), f32[16,1024]{1,0:T(8,128)}) %all-reduce.15.cloned.1.call-update) | async-done | bytes 65552 | tf_op jit(solution)/shard_map/psum | solution.py:110
  389.5 13.5 %all_gather.27 = bf16[64,1024]{1,0:T(8,128)(2,1)S(1)} all-gather(bf16[16,1024]{1,0:T(8,128)(2,1)S(1)} %multiply_convert_fusion), channel_id=1, replica_groups=mesh['section'=2,'req'=4,'head'=4] {'req'}, dimensions={0}, use_global_device_ids=true | all-gather | bytes 163840 | tf_op jit(solution)/shard_map/all_gather | solution.py:120
  406.9 7.2 %fusion = f32[64,1024]{1,0:T(8,128)} fusion(bf16[1,2816,1024]{2,1,0:T(8,128)(2,1)} %param.25, f32[64,2816]{1,0:T(8,128)S(1)} %fusion.69, bf16[64,1024]{1,0:T(8,128)(2,1)S(1)} %all_gather.27, bf16[1,1024,2816]{2,1,0:T(8,128)(2,1)} %param.24), kind=kOutput, calls=%fused_computation.2 | convolution fusion | flops 738557952 | bytes 12648448 | tf_op jit(solution)/shard_map/dot_general | solution.py:132
  414.1 19.8 %reduce-scatter.9.cloned.1.call-done = f32[16,1024]{1,0:T(8,128)} async-done(((f32[64,1024]{1,0:T(8,128)}), f32[16,1024]{1,0:T(8,128)}) %reduce-scatter.9.cloned.1.call-update) | async-done | bytes 65552 | tf_op jit(solution)/shard_map/reduce_scatter | solution.py:133
  434.0 42.5 %all-reduce.17.cloned.1.call-done = f32[16,1024]{1,0:T(8,128)} async-done(((f32[16,1024]{1,0:T(8,128)}), f32[16,1024]{1,0:T(8,128)}) %all-reduce.17.cloned.1.call-update) | async-done | bytes 65552 | tf_op jit(solution)/shard_map/psum | solution.py:134
  479.0 19.7 %reduce-scatter.11.cloned.1.call-done = bf16[32,1024]{1,0:T(8,128)(2,1)} async-done(((bf16[128,1024]{1,0:T(8,128)(2,1)}), bf16[32,1024]{1,0:T(8,128)(2,1)}) %reduce-scatter.11.cloned.1.call-update) | async-done | bytes 65552 | tf_op jit(solution)/shard_map/reduce_scatter | solution.py:145
  (144 shorter events, 59.6 us)
Async XLA Ops:
  6.5 43.0 %copy-start = (bf16[1,256,1024]{2,1,0:T(8,128)(2,1)S(1)}, bf16[1,256,1024]{2,1,0:T(8,128)(2,1)}, u32[]{:S(2)}) copy-start(bf16[1,256,1024]{2,1,0:T(8,128)(2,1)} %param.20) | copy-start | bytes 1572868
  6.5 87.0 %all-reduce.7.cloned.1.call-start = ((), (), s32[]{:S(2)}) async-start(), calls=%async_computation.4 | async-start | bytes 131072 | tf_op jit(solution)/shard_map/psum | solution.py:110
  7.9 18.4 %copy-start.5 = (f32[1,1024]{1,0:T(1,128)S(1)}, f32[1,1024]{1,0:T(1,128)}, u32[]{:S(2)}) copy-start(f32[1,1024]{1,0:T(1,128)} %param.21) | copy-start | bytes 12292
  36.3 3.9 copy-start.8
  47.0 3.5 copy-start.7
  47.0 3.6 copy-start.9
  47.0 47.6 %copy-start.6 = (f32[1,1024]{1,0:T(1,128)S(1)}, f32[1,1024]{1,0:T(1,128)}, u32[]{:S(2)}) copy-start(f32[1,1024]{1,0:T(1,128)} %param.22) | copy-start | bytes 12292
  50.4 89.5 %reduce-scatter.5.cloned.1.call-start = ((), (), s32[]{:S(2)}) async-start(), calls=%async_computation.5 | async-start | bytes 327680 | tf_op jit(solution)/shard_map/reduce_scatter | solution.py:133
  112.9 69.7 %copy-start.2 = (f32[16,1024]{1,0:T(8,128)S(1)}, f32[16,1024]{1,0:T(8,128)}, u32[]{:S(2)}) copy-start(f32[16,1024]{1,0:T(8,128)} %all-reduce.7.cloned.1.call-done) | copy-start | bytes 196612
  120.1 62.4 %all-reduce.9.cloned.1.call-start = ((), (), s32[]{:S(2)}) async-start(), calls=%async_computation.6 | async-start | bytes 131072 | tf_op jit(solution)/shard_map/psum | solution.py:134
  139.9 101.3 %all-reduce.11.cloned.1.call-start = ((), (), s32[]{:S(2)}) async-start(), calls=%async_computation.7 | async-start | bytes 131072 | tf_op jit(solution)/shard_map/psum | solution.py:110
  183.4 9.3 %collective-permute-start = (bf16[16,1024]{1,0:T(8,128)(2,1)S(1)}, bf16[16,1024]{1,0:T(8,128)(2,1)S(1)}, u32[]{:S(2)}, u32[]{:S(2)}) collective-permute-start(bf16[16,1024]{1,0:T(8,128)(2,1)S(1)} %get-tuple-element.15), channel_id=1, source_target_pairs={{0,16},{1,17},{2,18},{3,19},{4,20},{5,21},{6,22},{7,23},{8,24},{9,... | collective-permute-start | bytes 98312 | tf_op jit(solution)/shard_map/ppermute | solution.py:17
  199.6 87.9 %reduce-scatter.7.cloned.1.call-start = ((), (), s32[]{:S(2)}) async-start(), calls=%async_computation.8 | async-start | bytes 327680 | tf_op jit(solution)/shard_map/reduce_scatter | solution.py:133
  260.5 69.7 %copy-start.4 = (f32[16,1024]{1,0:T(8,128)S(1)}, f32[16,1024]{1,0:T(8,128)}, u32[]{:S(2)}) copy-start(f32[16,1024]{1,0:T(8,128)} %all-reduce.11.cloned.1.call-done) | copy-start | bytes 196612
  267.7 62.5 %all-reduce.13.cloned.1.call-start = ((), (), s32[]{:S(2)}) async-start(), calls=%async_computation.9 | async-start | bytes 131072 | tf_op jit(solution)/shard_map/psum | solution.py:134
  287.5 100.1 %all-reduce.15.cloned.1.call-start = ((), (), s32[]{:S(2)}) async-start(), calls=%async_computation.10 | async-start | bytes 131072 | tf_op jit(solution)/shard_map/psum | solution.py:110
  331.0 9.4 %collective-permute-start.1 = (bf16[16,1024]{1,0:T(8,128)(2,1)S(1)}, bf16[16,1024]{1,0:T(8,128)(2,1)S(1)}, u32[]{:S(2)}, u32[]{:S(2)}) collective-permute-start(bf16[16,1024]{1,0:T(8,128)(2,1)S(1)} %get-tuple-element.11), channel_id=1, source_target_pairs={{0,16},{1,17},{2,18},{3,19},{4,20},{5,21},{6,22},{7,23},{8,24},{9,... | collective-permute-start | bytes 98312 | tf_op jit(solution)/shard_map/ppermute | solution.py:17
  341.1 3.2 copy-start.1
  346.0 87.9 %reduce-scatter.9.cloned.1.call-start = ((), (), s32[]{:S(2)}) async-start(), calls=%async_computation.11 | async-start | bytes 327680 | tf_op jit(solution)/shard_map/reduce_scatter | solution.py:133
  406.9 69.6 %copy-start.3 = (f32[16,1024]{1,0:T(8,128)S(1)}, f32[16,1024]{1,0:T(8,128)}, u32[]{:S(2)}) copy-start(f32[16,1024]{1,0:T(8,128)} %all-reduce.15.cloned.1.call-done) | copy-start | bytes 196612
  414.1 62.4 %all-reduce.17.cloned.1.call-start = ((), (), s32[]{:S(2)}) async-start(), calls=%async_computation.12 | async-start | bytes 131072 | tf_op jit(solution)/shard_map/psum | solution.py:134
  433.9 64.8 %reduce-scatter.11.cloned.1.call-start = ((), (), s32[]{:S(2)}) async-start(), calls=%async_computation.13 | async-start | bytes 327680 | tf_op jit(solution)/shard_map/reduce_scatter | solution.py:145
Sparse Core Ops, SparseCore 0:
  50.5 43.0 all-reduce.6
  120.2 19.6 reduce-scatter.4
  142.8 39.6 all-reduce.8
  199.7 41.4 all-reduce.10
  267.8 19.6 reduce-scatter.6
  290.4 39.7 all-reduce.12
  346.1 41.4 all-reduce.14
  414.2 19.6 reduce-scatter.8
  436.8 39.6 all-reduce.16
  479.1 19.5 reduce-scatter.10
where the time goes:
time: 507 us; the launch traced here: 506 us
  waiting for transfers between devices  293 us (58%)
  blocking collectives  95.8 us (19%)
  matrix products  48.3 us (10%)
  local copies, waits for them, and re-layouts  37.2 us (7%)
  other arithmetic  14 us (3%)
  between operations  13.9 us (3%)
    psum x3, waiting for transfers between devices, on_device(): mixture = lax.psum(mixture, 'head')  128 us
    psum x3, waiting for transfers between devices, on_device(): attention = lax.psum(partial_value, 'head')  86.3 us
    all_gather x6, blocking collectives, on_device(): lax.all_gather((normed_ffn, combine), 'req', axis=0, tiled=True)  79.9 us
    reduce_scatter x3, waiting for transfers between devices, on_device(): lax.psum_scatter(partial_terms, 'req', scatter_dimension=0, tiled=True)  59.3 us
    unnamed x27, local copies, waits for them, and re-layouts  25.3 us
    dot_general x3, matrix products, on_device(): jnp.dot(hidden, w_down[0], preferred_element_type=jnp.float32)  21.5 us
    reduce_scatter x1, waiting for transfers between devices, on_device(): lax.psum_scatter(placed.astype(jnp.bfloat16), 'req', scatter_dimension=0,...  19.7 us
    all_gather x1, blocking collectives, on_device(): everything = lax.all_gather(tokens, 'req', axis=0, tiled=True)  15.8 us
  transfers between devices with their start and end apart: 12, of which 10 were waited for; matrix products, arithmetic and copies ran while one was open for 3% of the time, Pallas kernels for 0%

commit v1 on v0

--- a/solution.py
+++ b/solution.py
@@ -131,7 +131,7 @@
         ).astype(jnp.bfloat16)
         partial_terms = jnp.dot(hidden, w_down[0], preferred_element_type=jnp.float32)
         mixture = lax.psum_scatter(partial_terms, "req", scatter_dimension=0, tiled=True)
-        mixture = lax.psum(mixture, "head")
+        mixture = jnp.sum(lax.all_gather(mixture, "head"), axis=0)
         produced = (residual + mixture).astype(jnp.bfloat16)
         updated = lax.dynamic_update_slice_in_dim(results, produced, clamped * block_rows, 0)
         results = jnp.where(in_window, updated, results)

time: 507 us -> 398 us (0.79)
  waiting for transfers between devices: 293 us -> 158 us
  blocking collectives: 95.8 us -> 124 us
    psum x3 -> x0, waiting for transfers between devices: 128 us -> none  [on_device(): mixture = lax.psum(mixture, 'head')]
    all_gather x0 -> x3, blocking collectives: none -> 28.1 us  [on_device(): mixture = jnp.sum(lax.all_gather(mixture, 'head'), axis=0)]
    psum x3, waiting for transfers between devices: 86.3 us -> 81.1 us  [on_device(): attention = lax.psum(partial_value, 'head')]
    unnamed x27 -> x25, local copies, waits for them, and re-layouts: 25.3 us -> 25.3 us
  transfers between devices with their start and end apart: 12 -> 9, of which waited for: 10 -> 7; matrix products, arithmetic and copies ran while one was open for 3% -> 4% of each run, Pallas kernels for 0% -> 0%
where the time goes in v1:
time: 398 us; the launch traced here: 397 us
  waiting for transfers between devices  158 us (40%)
  blocking collectives  124 us (31%)
  matrix products  49.7 us (12%)
  local copies, waits for them, and re-layouts  37.2 us (9%)
  between operations  13.9 us (3%)
  other arithmetic  11.5 us (3%)
    psum x3, waiting for transfers between devices, on_device(): attention = lax.psum(partial_value, 'head')  81.1 us
    all_gather x6, blocking collectives, on_device(): lax.all_gather((normed_ffn, combine), 'req', axis=0, tiled=True)  79.9 us
    reduce_scatter x3, waiting for transfers between devices, on_device(): lax.psum_scatter(partial_terms, 'req', scatter_dimension=0, tiled=True)  59.3 us
    all_gather x3, blocking collectives, on_device(): mixture = jnp.sum(lax.all_gather(mixture, 'head'), axis=0)  28.1 us
    unnamed x25, local copies, waits for them, and re-layouts  25.3 us
    dot_general x3, matrix products, on_device(): jnp.dot(hidden, w_down[0], preferred_element_type=jnp.float32)  21.5 us
    reduce_scatter x1, waiting for transfers between devices, on_device(): lax.psum_scatter(placed.astype(jnp.bfloat16), 'req', scatter_dimension=0,...  17.2 us
    all_gather x1, blocking collectives, on_device(): everything = lax.all_gather(tokens, 'req', axis=0, tiled=True)  15.8 us
  transfers between devices with their start and end apart: 9, of which 7 were waited for; matrix products, arithmetic and copies ran while one was open for 4% of the time, Pallas kernels for 0%

profile of v1, /device:TPU:0, one launch (start us, length us, event | category | flops | bytes accessed | tf_op | source)
XLA Modules:
  0.0 396.9 jit_solution(4974789988614014061)
XLA Ops:
  7.9 15.8 %all_gather.39 = bf16[128,1024]{1,0:T(8,128)(2,1)S(1)} all-gather(bf16[32,1024]{1,0:T(8,128)(2,1)} %param.14), channel_id=1, replica_groups=mesh['section'=2,'req'=4,'head'=4] {'req'}, dimensions={0}, use_global_device_ids=true | all-gather | bytes 327680 | tf_op jit(solution)/shard_map/all_gather | solution.py:79
  27.1 9.2 %constant_dynamic-slice_fusion.2 = (bf16[1,16,256,256]{3,2,1,0:T(8,128)(2,1)}, bf16[1,16,256,256]{3,2,1,0:T(8,128)(2,1)}, bf16[1,16,256,256]{3,2,1,0:T(8,128)(2,...) fusion(bf16[1,32,256,256]{3,2,1,0:T(8,128)(2,1)} %param.18, ...), kind=kLoop, calls=%fused_computation.162 | loop fusion | bytes 25165836 | tf_op jit(solution)/shard_map/dynamic_slice | solution.py:94
  43.0 3.9 copy.79
  50.7 13.2 %all_gather.40 = bf16[64,16]{1,0:T(8,128)(2,1)S(1)} all-gather(bf16[16,16]{1,0:T(8,128)(2,1)S(1)} %fusion.130), channel_id=1, replica_groups=mesh['section'=2,'req'=4,'head'=4] {'req'}, dimensions={0}, use_global_device_ids=true | all-gather | bytes 2560 | tf_op jit(solution)/shard_map/all_gather | solution.py:120
  64.0 13.1 %all_gather.44 = bf16[64,16]{1,0:T(8,128)(2,1)S(1)} all-gather(bf16[16,16]{1,0:T(8,128)(2,1)S(1)} %fusion.129), channel_id=1, replica_groups=mesh['section'=2,'req'=4,'head'=4] {'req'}, dimensions={0}, use_global_device_ids=true | all-gather | bytes 2560 | tf_op jit(solution)/shard_map/all_gather | solution.py:120
  77.2 13.1 %all_gather.48 = bf16[64,16]{1,0:T(8,128)(2,1)S(1)} all-gather(bf16[16,16]{1,0:T(8,128)(2,1)S(1)} %fusion.128), channel_id=1, replica_groups=mesh['section'=2,'req'=4,'head'=4] {'req'}, dimensions={0}, use_global_device_ids=true | all-gather | bytes 2560 | tf_op jit(solution)/shard_map/all_gather | solution.py:120
  95.5 13.5 %all_gather.41 = bf16[64,1024]{1,0:T(8,128)(2,1)S(1)} all-gather(bf16[16,1024]{1,0:T(8,128)(2,1)S(1)} %multiply_convert_fusion.2), channel_id=1, replica_groups=mesh['section'=2,'req'=4,'head'=4] {'req'}, dimensions={0}, use_global_device_ids=true | all-gather | bytes 163840 | tf_op jit(solution)/shard_map/all_gather | solution.py:120
  112.9 7.2 %fusion.4 = f32[64,1024]{1,0:T(8,128)} fusion(bf16[1,2816,1024]{2,1,0:T(8,128)(2,1)} %param.25, f32[64,2816]{1,0:T(8,128)S(1)} %fusion.45, bf16[64,1024]{1,0:T(8,128)(2,1)S(1)} %all_gather.41, bf16[1,1024,2816]{2,1,0:T(8,128)(2,1)} %param.24), kind=kOutput, calls=%fused_computation.6 | convolution fusion | flops 738557952 | bytes 12648448 | tf_op jit(solution)/shard_map/dot_general | solution.py:132
  120.1 19.8 %reduce-scatter.5.cloned.1.call-done = f32[16,1024]{1,0:T(8,128)} async-done(((f32[64,1024]{1,0:T(8,128)}), f32[16,1024]{1,0:T(8,128)}) %reduce-scatter.5.cloned.1.call-update) | async-done | bytes 65552 | tf_op jit(solution)/shard_map/reduce_scatter | solution.py:133
  139.9 9.4 %all-gather = f32[64,1024]{1,0:T(8,128)S(1)} all-gather(f32[16,1024]{1,0:T(8,128)} %reduce-scatter.5.cloned.1.call-done), channel_id=2, replica_groups=mesh['section'=2,'req'=4,'head'=4] {'head'}, dimensions={0}, use_global_device_ids=true | all-gather | bytes 327680 | tf_op jit(solution)/shard_map/all_gather | solution.py:134
  154.6 3.9 copy.81
  165.5 39.0 %all-reduce.6.cloned.1.call-done = f32[16,1024]{1,0:T(8,128)} async-done(((f32[16,1024]{1,0:T(8,128)}), f32[16,1024]{1,0:T(8,128)}) %all-reduce.6.cloned.1.call-update) | async-done | bytes 65552 | tf_op jit(solution)/shard_map/psum | solution.py:110
  206.4 13.5 %all_gather.45 = bf16[64,1024]{1,0:T(8,128)(2,1)S(1)} all-gather(bf16[16,1024]{1,0:T(8,128)(2,1)S(1)} %multiply_convert_fusion.1), channel_id=1, replica_groups=mesh['section'=2,'req'=4,'head'=4] {'req'}, dimensions={0}, use_global_device_ids=true | all-gather | bytes 163840 | tf_op jit(solution)/shard_map/all_gather | solution.py:120
  223.8 7.2 %fusion.2 = f32[64,1024]{1,0:T(8,128)} fusion(bf16[1,2816,1024]{2,1,0:T(8,128)(2,1)} %param.25, f32[64,2816]{1,0:T(8,128)S(1)} %fusion.57, bf16[64,1024]{1,0:T(8,128)(2,1)S(1)} %all_gather.45, bf16[1,1024,2816]{2,1,0:T(8,128)(2,1)} %param.24), kind=kOutput, calls=%fused_computation.4 | convolution fusion | flops 738557952 | bytes 12648448 | tf_op jit(solution)/shard_map/dot_general | solution.py:132
  231.0 19.8 %reduce-scatter.7.cloned.1.call-done = f32[16,1024]{1,0:T(8,128)} async-done(((f32[64,1024]{1,0:T(8,128)}), f32[16,1024]{1,0:T(8,128)}) %reduce-scatter.7.cloned.1.call-update) | async-done | bytes 65552 | tf_op jit(solution)/shard_map/reduce_scatter | solution.py:133
  250.8 9.4 %all-gather.1 = f32[64,1024]{1,0:T(8,128)S(1)} all-gather(f32[16,1024]{1,0:T(8,128)} %reduce-scatter.7.cloned.1.call-done), channel_id=3, replica_groups=mesh['section'=2,'req'=4,'head'=4] {'head'}, dimensions={0}, use_global_device_ids=true | all-gather | bytes 327680 | tf_op jit(solution)/shard_map/all_gather | solution.py:134
  261.7 3.9 copy.82
  265.6 3.9 copy.83
  276.6 38.9 %all-reduce.8.cloned.1.call-done = f32[16,1024]{1,0:T(8,128)} async-done(((f32[16,1024]{1,0:T(8,128)}), f32[16,1024]{1,0:T(8,128)}) %all-reduce.8.cloned.1.call-update) | async-done | bytes 65552 | tf_op jit(solution)/shard_map/psum | solution.py:110
  317.4 13.5 %all_gather.49 = bf16[64,1024]{1,0:T(8,128)(2,1)S(1)} all-gather(bf16[16,1024]{1,0:T(8,128)(2,1)S(1)} %multiply_convert_fusion), channel_id=1, replica_groups=mesh['section'=2,'req'=4,'head'=4] {'req'}, dimensions={0}, use_global_device_ids=true | all-gather | bytes 163840 | tf_op jit(solution)/shard_map/all_gather | solution.py:120
  334.8 7.2 %fusion = f32[64,1024]{1,0:T(8,128)} fusion(bf16[1,2816,1024]{2,1,0:T(8,128)(2,1)} %param.25, f32[64,2816]{1,0:T(8,128)S(1)} %fusion.69, bf16[64,1024]{1,0:T(8,128)(2,1)S(1)} %all_gather.49, bf16[1,1024,2816]{2,1,0:T(8,128)(2,1)} %param.24), kind=kOutput, calls=%fused_computation.2 | convolution fusion | flops 738557952 | bytes 12648448 | tf_op jit(solution)/shard_map/dot_general | solution.py:132
  342.0 19.8 %reduce-scatter.9.cloned.1.call-done = f32[16,1024]{1,0:T(8,128)} async-done(((f32[64,1024]{1,0:T(8,128)}), f32[16,1024]{1,0:T(8,128)}) %reduce-scatter.9.cloned.1.call-update) | async-done | bytes 65552 | tf_op jit(solution)/shard_map/reduce_scatter | solution.py:133
  361.8 9.4 %all-gather.2 = f32[64,1024]{1,0:T(8,128)S(1)} all-gather(f32[16,1024]{1,0:T(8,128)} %reduce-scatter.9.cloned.1.call-done), channel_id=4, replica_groups=mesh['section'=2,'req'=4,'head'=4] {'head'}, dimensions={0}, use_global_device_ids=true | all-gather | bytes 327680 | tf_op jit(solution)/shard_map/all_gather | solution.py:134
  372.8 17.2 %reduce-scatter.11.cloned.1.call-done = bf16[32,1024]{1,0:T(8,128)(2,1)} async-done(((bf16[128,1024]{1,0:T(8,128)(2,1)}), bf16[32,1024]{1,0:T(8,128)(2,1)}) %reduce-scatter.11.cloned.1.call-update) | async-done | bytes 65552 | tf_op jit(solution)/shard_map/reduce_scatter | solution.py:145
  (139 shorter events, 58.2 us)
Async XLA Ops:
  6.5 43.0 %copy-start = (bf16[1,256,1024]{2,1,0:T(8,128)(2,1)S(1)}, bf16[1,256,1024]{2,1,0:T(8,128)(2,1)}, u32[]{:S(2)}) copy-start(bf16[1,256,1024]{2,1,0:T(8,128)(2,1)} %param.20) | copy-start | bytes 1572868
  6.5 87.0 %all-reduce.4.cloned.1.call-start = ((), (), s32[]{:S(2)}) async-start(), calls=%async_computation.4 | async-start | bytes 131072 | tf_op jit(solution)/shard_map/psum | solution.py:110
  7.9 18.4 %copy-start.4 = (f32[1,1024]{1,0:T(1,128)S(1)}, f32[1,1024]{1,0:T(1,128)}, u32[]{:S(2)}) copy-start(f32[1,1024]{1,0:T(1,128)} %param.21) | copy-start | bytes 12292
  36.3 3.9 copy-start.7
  47.0 3.5 copy-start.6
  47.0 3.6 copy-start.8
  47.0 47.6 %copy-start.5 = (f32[1,1024]{1,0:T(1,128)S(1)}, f32[1,1024]{1,0:T(1,128)}, u32[]{:S(2)}) copy-start(f32[1,1024]{1,0:T(1,128)} %param.22) | copy-start | bytes 12292
  50.4 89.5 %reduce-scatter.5.cloned.1.call-start = ((), (), s32[]{:S(2)}) async-start(), calls=%async_computation.5 | async-start | bytes 327680 | tf_op jit(solution)/shard_map/reduce_scatter | solution.py:133
  112.9 36.4 %copy-start.1 = (f32[16,1024]{1,0:T(8,128)S(1)}, f32[16,1024]{1,0:T(8,128)}, u32[]{:S(2)}) copy-start(f32[16,1024]{1,0:T(8,128)} %all-reduce.4.cloned.1.call-done) | copy-start | bytes 196612
  120.1 84.5 %all-reduce.6.cloned.1.call-start = ((), (), s32[]{:S(2)}) async-start(), calls=%async_computation.6 | async-start | bytes 131072 | tf_op jit(solution)/shard_map/psum | solution.py:110
  149.3 9.2 %collective-permute-start = (bf16[16,1024]{1,0:T(8,128)(2,1)S(1)}, bf16[16,1024]{1,0:T(8,128)(2,1)S(1)}, u32[]{:S(2)}, u32[]{:S(2)}) collective-permute-start(bf16[16,1024]{1,0:T(8,128)(2,1)S(1)} %get-tuple-element.15), channel_id=1, source_target_pairs={{0,16},{1,17},{2,18},{3,19},{4,20},{5,21},{6,22},{7,23},{8,24},{9,... | collective-permute-start | bytes 98312 | tf_op jit(solution)/shard_map/ppermute | solution.py:17
  165.5 85.3 %reduce-scatter.7.cloned.1.call-start = ((), (), s32[]{:S(2)}) async-start(), calls=%async_computation.7 | async-start | bytes 327680 | tf_op jit(solution)/shard_map/reduce_scatter | solution.py:133
  223.8 36.4 %copy-start.3 = (f32[16,1024]{1,0:T(8,128)S(1)}, f32[16,1024]{1,0:T(8,128)}, u32[]{:S(2)}) copy-start(f32[16,1024]{1,0:T(8,128)} %all-reduce.6.cloned.1.call-done) | copy-start | bytes 196612
  231.0 84.5 %all-reduce.8.cloned.1.call-start = ((), (), s32[]{:S(2)}) async-start(), calls=%async_computation.8 | async-start | bytes 131072 | tf_op jit(solution)/shard_map/psum | solution.py:110
  260.2 9.3 %collective-permute-start.1 = (bf16[16,1024]{1,0:T(8,128)(2,1)S(1)}, bf16[16,1024]{1,0:T(8,128)(2,1)S(1)}, u32[]{:S(2)}, u32[]{:S(2)}) collective-permute-start(bf16[16,1024]{1,0:T(8,128)(2,1)S(1)} %get-tuple-element.11), channel_id=1, source_target_pairs={{0,16},{1,17},{2,18},{3,19},{4,20},{5,21},{6,22},{7,23},{8,24},{9,... | collective-permute-start | bytes 98312 | tf_op jit(solution)/shard_map/ppermute | solution.py:17
  276.5 85.3 %reduce-scatter.9.cloned.1.call-start = ((), (), s32[]{:S(2)}) async-start(), calls=%async_computation.9 | async-start | bytes 327680 | tf_op jit(solution)/shard_map/reduce_scatter | solution.py:133
  334.8 36.4 %copy-start.2 = (f32[16,1024]{1,0:T(8,128)S(1)}, f32[16,1024]{1,0:T(8,128)}, u32[]{:S(2)}) copy-start(f32[16,1024]{1,0:T(8,128)} %all-reduce.8.cloned.1.call-done) | copy-start | bytes 196612
  342.0 48.1 %reduce-scatter.11.cloned.1.call-start = ((), (), s32[]{:S(2)}) async-start(), calls=%async_computation.10 | async-start | bytes 327680 | tf_op jit(solution)/shard_map/reduce_scatter | solution.py:145
Sparse Core Ops, SparseCore 0:
  50.5 43.0 all-reduce.3
  120.2 19.6 reduce-scatter.4
  165.6 38.8 all-reduce.5
  231.1 19.6 reduce-scatter.6
  276.6 38.8 all-reduce.7
  342.1 19.6 reduce-scatter.8
  372.9 17.0 reduce-scatter.10
